TPU v7x, 768 devices: a whole 4x8x12 slice. The times are simulated.
768 devices in a mesh: energy: 12 (over z), elem: 32 (over y, x), space: 2 (over core).
Axes of the slice: x: 4, y: 8, z: 12, core: 2. Of those that a mesh axis runs over, the one named last changes fastest.
Arguments:
- cell_blocks: float32 [4, 256, 256], P('space'), may hold values from -4 to 23, as said below
- coupling_blocks: float32 [4, 256, 256], P('space'), may hold values from -1 to 5
- sigma_prev: bfloat16 [384, 4, 256, 256], P(('energy', 'elem'), 'space'), may hold values from -1 to 3, as said below
- shifts: int32 [4], replicated, may hold values from 1 to 32, as said below
- strengths: float32 [4], replicated, may hold values from 0.5 to 2
Outputs:
- sigma_next: float32 [384, 4, 256, 256], P('energy', 'space', 'elem')
Inputs may be any that keep to these rules, and one draw needn't show every extreme that they name: `cell_blocks`: each block is symmetric. `sigma_prev`: each block is symmetric; every M and every X(i) of the steps is positive definite. `shifts`: one branch's offset equals 32.
All inputs are finite; a program needn't handle non-finite values.
Results may differ from a plain program's by a relative error of at most 0.0003.
Values sent between devices are 32-bit elements; how exact they have to be, the bound alone decides.
No kernel may reach another device: no remote copies, remote signals or barrier semaphores. Data moves between devices by JAX's collectives and lax.ppermute only.
A program may use at most 32 MiB of HBM per device.

v0:
```python
import functools

import jax
import jax.numpy as jnp
from jax import lax
from jax.experimental import pallas as pl
from jax.experimental.pallas import tpu as pltpu
from jax.sharding import PartitionSpec as P

MODES = 4
LEVEL_STEP = 3.0 / 384.0
RESIDUAL_MAX = 1e-3

f32 = jnp.float32
bf16 = jnp.bfloat16


def parts_of(matrix):
    high = matrix.astype(bf16)
    return high, (matrix - high.astype(f32)).astype(bf16)


def product_1(left, right):
    return jnp.dot(left, right, preferred_element_type=f32)


def product_3(left, right):
    return product_1(left[0], right[0]) + (
        product_1(left[1], right[0]) + product_1(left[0], right[1])
    )


def product_full(left, right):
    return jnp.dot(left, right, preferred_element_type=f32, precision=lax.Precision.HIGHEST)


def diagonal_mask(size):
    rows = lax.broadcasted_iota(jnp.int32, (size, size), 0)
    columns = lax.broadcasted_iota(jnp.int32, (size, size), 1)
    return rows == columns


def invert_series(matrix, diagonal):
    size = matrix.shape[0]
    mass = jnp.sum(jnp.where(diagonal, matrix, 0.0), axis=0, keepdims=True)
    scale = size / jnp.sum(mass, axis=1, keepdims=True)
    one = jnp.where(diagonal, 1.0, 0.0).astype(f32)
    rest = one - matrix * scale
    rest_parts = parts_of(rest)
    rest_2 = product_1(rest_parts[0], rest_parts[0])
    rest_2b = rest_2.astype(bf16)
    rest_3 = product_1(rest_parts[0], rest_2b)
    rest_4 = product_1(rest_2b, rest_2b)
    tail = rest + rest_2 + rest_3
    tail = tail + rest_4 + product_1(tail.astype(bf16), rest_4.astype(bf16))
    tail_parts = parts_of(tail)
    residual = rest - tail + product_3(rest_parts, tail_parts)
    tail = tail + residual + product_1(tail_parts[0], residual.astype(bf16))
    squared = jnp.sum(jnp.sum(residual * residual, axis=0, keepdims=True), axis=1, keepdims=True)
    return scale * (one + tail), squared


def invert_direct(matrix, diagonal, work):
    size = matrix.shape[0]
    rows = lax.broadcasted_iota(jnp.int32, (size, size), 0)
    columns = lax.broadcasted_iota(jnp.int32, (size, size), 1)
    work[...] = matrix

    def eliminate(pivot, _):
        values = work[...]
        row = work[pl.ds(pivot, 1), :]
        on_row, on_column = (rows == pivot, columns == pivot)
        column = jnp.sum(jnp.where(on_column, values, 0.0), axis=1, keepdims=True)
        corner = jnp.sum(jnp.where(on_column[:1], row, 0.0), axis=1, keepdims=True)
        scaled = row / corner
        updated = jnp.where(on_column, -column / corner, values - column * scaled)
        pivot_row = jnp.where(on_column[:1], 1.0 / corner, scaled)
        work[...] = jnp.where(on_row, pivot_row, updated)
        return 0

    lax.fori_loop(0, size, eliminate, 0)
    inverse = work[...]
    one = jnp.where(diagonal, 1.0, 0.0).astype(f32)
    return inverse + product_full(inverse, one - product_full(matrix, inverse))


def symmetric(matrix):
    return 0.5 * (matrix + matrix.T)


def eliminate_kernel(
    cell_ref, coupling_ref, sigma_ref, sum_ref, first_ref, fold_ref, second_ref, far_ref, work
):
    part = lax.axis_index("space")
    position = lax.axis_index("energy") * lax.axis_size("elem") + lax.axis_index("elem")
    level = position.astype(f32) * LEVEL_STEP
    near = part == 0
    size = cell_ref.shape[-1]
    diagonal = diagonal_mask(size)

    def block(index):
        return cell_ref[index] + jnp.where(diagonal, level, 0.0) + sigma_ref[0, index].astype(f32)

    def chain(invert, product, parts):
        outer, inner, last = (block(part), block(0), block(1))
        link = coupling_ref[part]
        link_turned = link.T
        link, link_turned = (
            jnp.where(near, link, link_turned), jnp.where(near, link_turned, link)
        )
        inner_link = coupling_ref[1 - part]
        inner_turned = inner_link.T
        inner_link, inner_turned = (
            jnp.where(near, inner_link, inner_turned), jnp.where(near, inner_turned, inner_link)
        )
        first, error = invert(outer)
        fold = product(parts(first), parts(link))
        second, error_second = invert(inner - product(parts(link_turned), parts(fold)))
        far = product(parts(second), parts(inner_link))
        total = jnp.where(near, last, 0.0) - product(parts(inner_turned), parts(far))
        first_ref[...] = first
        fold_ref[...] = fold
        second_ref[...] = second
        far_ref[...] = far
        sum_ref[...] = total
        return jnp.maximum(error, error_second)

    error = chain(lambda m: invert_series(m, diagonal), product_3, parts_of)

    @pl.when(jnp.logical_not(error[0, 0] <= RESIDUAL_MAX))
    def _():
        chain(
            lambda m: (invert_direct(m, diagonal, work), jnp.zeros((1, 1), f32)),
            product_full,
            lambda m: m,
        )


def recover_kernel(own_ref, other_ref, first_ref, fold_ref, second_ref, far_ref, green_ref, work):
    near = lax.axis_index("space") == 0
    size = own_ref.shape[-1]
    diagonal = diagonal_mask(size)
    groups, _, rows, _ = green_ref.shape

    def chain(invert, product, parts):
        middle, error = invert(own_ref[...] + other_ref[...])
        middle = symmetric(middle)
        far = far_ref[...]
        second = symmetric(
            second_ref[...] + product(parts(product(parts(far), parts(middle))), parts(far.T))
        )
        green_ref[:, 0] = second.reshape(groups, rows, size)

        @pl.when(near)
        def _():
            green_ref[:, 1] = middle.reshape(groups, rows, size)

        @pl.when(jnp.logical_not(near))
        def _():
            fold = fold_ref[...]
            outer = symmetric(
                first_ref[...] + product(parts(product(parts(fold), parts(second))), parts(fold.T))
            )
            green_ref[:, 1] = outer.reshape(groups, rows, size)

        return error

    error = chain(lambda m: invert_series(m, diagonal), product_3, parts_of)

    @pl.when(jnp.logical_not(error[0, 0] <= RESIDUAL_MAX))
    def _():
        chain(
            lambda m: (invert_direct(m, diagonal, work), jnp.zeros((1, 1), f32)),
            product_full,
            lambda m: m,
        )


def spread_kernel(shifts_ref, strengths_ref, below_ref, own_ref, above_ref, out_ref, rim, sems):
    width = own_ref.shape[0]
    copies = [
        pltpu.make_async_copy(source, rim.at[pl.ds(place * width, width)], sems.at[place])
        for place, source in enumerate((below_ref, own_ref, above_ref))
    ]
    for copy in copies:
        copy.start()
    for copy in copies:
        copy.wait()

    def one(index, _):
        total = None
        for phonon in range(MODES):
            shift = shifts_ref[phonon]
            term = strengths_ref[phonon] * (rim[width + index - shift] + rim[width + index + shift])
            total = term if total is None else total + term
        out_ref[index] = total
        return 0

    lax.fori_loop(0, width, one, 0, unroll=4)


def body(cell_blocks, coupling_blocks, sigma_prev, shifts, strengths):
    orbitals = sigma_prev.shape[2]
    elem_size = lax.axis_size("elem")
    square = jax.ShapeDtypeStruct((orbitals, orbitals), f32)
    vmem = pl.BlockSpec(memory_space=pltpu.VMEM)
    smem = pl.BlockSpec(memory_space=pltpu.SMEM)
    anywhere = pl.BlockSpec(memory_space=pl.ANY)
    own, first, fold, second, far = pl.pallas_call(
        eliminate_kernel,
        out_shape=[square] * 5,
        in_specs=[vmem] * 3,
        out_specs=[vmem] * 5,
        scratch_shapes=[pltpu.VMEM((orbitals, orbitals), f32)],
    )(cell_blocks, coupling_blocks, sigma_prev)
    other = lax.ppermute(own, "space", [(0, 1), (1, 0)])
    green = pl.pallas_call(
        recover_kernel,
        out_shape=jax.ShapeDtypeStruct((elem_size, 2, orbitals // elem_size, orbitals), f32),
        in_specs=[vmem] * 6,
        out_specs=vmem,
        scratch_shapes=[pltpu.VMEM((orbitals, orbitals), f32)],
    )(own, other, first, fold, second, far)
    arrived = lax.all_to_all(green, "elem", split_axis=0, concat_axis=0, tiled=True)
    ends = lax.axis_size("energy") - 1
    below = lax.ppermute(arrived, "energy", [(i, i + 1) for i in range(ends)])
    above = lax.ppermute(arrived, "energy", [(i + 1, i) for i in range(ends)])
    width = arrived.shape[0]
    return pl.pallas_call(
        spread_kernel,
        out_shape=jax.ShapeDtypeStruct(arrived.shape, f32),
        in_specs=[smem, smem, anywhere, anywhere, anywhere],
        out_specs=vmem,
        scratch_shapes=[
            pltpu.VMEM((3 * width,) + arrived.shape[1:], f32),
            pltpu.SemaphoreType.DMA((3,)),
        ],
    )(shifts, strengths, below, arrived, above)


def solution(mesh):
    in_specs = (
        P("space", None, None),
        P("space", None, None),
        P(("energy", "elem"), "space", None, None),
        P(),
        P(),
    )
    out_specs = P("energy", "space", "elem", None)
    return jax.shard_map(body, mesh=mesh, in_specs=in_specs, out_specs=out_specs, check_vma=False)
```

profile of v0, /device:TPU:66, one launch (start us, length us, event | category | flops | bytes accessed | tf_op | source)
XLA Modules:
  0.0 66.7 jit_solution(14314722265951571099)
XLA Ops:
  0.0 5.9 %shard_map.55 = (f32[256,256]{1,0:T(8,128)}, f32[256,256]{1,0:T(8,128)}, f32[256,256]{1,0:T(8,128)}, f32[256,256]{1,0:T(8,128)}, f32[256,256]{1,0:T(8,128)}) custom-call(f32[2,256,256]{2,1,0:T(8,128)} %cell_ref.1, f32[2,256,256]{2,1,0:T(8,128)} %coupling_ref.1, bf16[1,2,256,256]{3,2,1,0:T(8,128)(2,1)} %sigma_ref.1), custom_call_target="tpu_custom_call" | custom-call | tf_op jit(solution)/shard_map/pallas_call | solution.py:209
  5.9 1.9 %collective-permute-start = (f32[256,256]{1,0:T(8,128)}, f32[256,256]{1,0:T(8,128)S(1)}, u32[]{:S(2)}, u32[]{:S(2)}) collective-permute-start(f32[256,256]{1,0:T(8,128)} %get-tuple-element.10.own_ref), channel_id=1, source_target_pairs={{0,1},{1,0},{2,3},{3,2},{4,5},{5,4},{6,7},{7,6},{8,9},{9,8},{10,11... | collective-permute-start | bytes 786440 | tf_op jit(solution)/shard_map/ppermute | solution.py:216
  7.9 1.7 %collective-permute-done.other_ref = f32[256,256]{1,0:T(8,128)S(1)} collective-permute-done((f32[256,256]{1,0:T(8,128)}, f32[256,256]{1,0:T(8,128)S(1)}, u32[]{:S(2)}, u32[]{:S(2)}) %collective-permute-start) | collective-permute-done | bytes 262176 | tf_op jit(solution)/shard_map/ppermute | solution.py:216
  9.6 0.0 copy-start.3
  9.6 0.7 %copy-done.3 = f32[256,256]{1,0:T(8,128)} copy-done((f32[256,256]{1,0:T(8,128)}, f32[256,256]{1,0:T(8,128)S(1)}, u32[]{:S(2)}) %copy-start.3) | copy-done | bytes 262168
  10.3 4.2 %shard_map.56 = f32[32,2,8,256]{3,2,1,0:T(8,128)} custom-call(f32[256,256]{1,0:T(8,128)} %get-tuple-element.10.own_ref, f32[256,256]{1,0:T(8,128)} %copy-done.3, f32[256,256]{1,0:T(8,128)} %get-tuple-element.11.first_ref, f32[256,256]{1,0:T(8,128)} %get-tuple-element.12.fold_ref, f32[256,256]{1,0:T(8,128)} %get-tuple-element.13.second_ref, ...), custom_call_target="tpu_custom_call" | custom-call | tf_op jit(solution)/shard_map/pallas_call | solution.py:217
  14.4 28.1 %all_to_all.5.own_ref = f32[32,2,8,256]{3,2,1,0:T(8,128)S(1)} all-to-all(f32[32,2,8,256]{3,2,1,0:T(8,128)} %shard_map.56), channel_id=1, replica_groups=mesh['energy'=12,'elem'=32,'space'=2] {'elem'}, dimensions={0} | all-to-all | bytes 1048576 | tf_op jit(solution)/shard_map/all_to_all | solution.py:224
  42.5 0.0 copy-start
  42.5 4.7 %collective-permute-start.2 = (f32[32,2,8,256]{3,2,1,0:T(8,128)S(1)}, f32[32,2,8,256]{3,2,1,0:T(8,128)S(1)}, u32[]{:S(2)}, u32[]{:S(2)}) collective-permute-start(f32[32,2,8,256]{3,2,1,0:T(8,128)S(1)} %all_to_all.5.own_ref), channel_id=1, source_target_pairs={{64,0},{128,64},{192,128},{256,192},{320,256},{384,320},{448,384},... | collective-permute-start | bytes 1572872 | tf_op jit(solution)/shard_map/ppermute | solution.py:227
  47.2 1.9 %collective-permute-start.1 = (f32[32,2,8,256]{3,2,1,0:T(8,128)S(1)}, f32[32,2,8,256]{3,2,1,0:T(8,128)S(1)}, u32[]{:S(2)}, u32[]{:S(2)}) collective-permute-start(f32[32,2,8,256]{3,2,1,0:T(8,128)S(1)} %all_to_all.5.own_ref), channel_id=1, source_target_pairs={{0,64},{64,128},{128,192},{192,256},{256,320},{320,384},{384,448},... | collective-permute-start | bytes 1572872 | tf_op jit(solution)/shard_map/ppermute | solution.py:226
  49.2 9.5 %collective-permute-done.2.above_ref = f32[32,2,8,256]{3,2,1,0:T(8,128)S(1)} collective-permute-done((f32[32,2,8,256]{3,2,1,0:T(8,128)S(1)}, f32[32,2,8,256]{3,2,1,0:T(8,128)S(1)}, u32[]{:S(2)}, u32[]{:S(2)}) %collective-permute-start.2) | collective-permute-done | bytes 524320 | tf_op jit(solution)/shard_map/ppermute | solution.py:227
  58.6 0.0 copy-start.1
  58.6 4.1 %collective-permute-done.1.below_ref = f32[32,2,8,256]{3,2,1,0:T(8,128)S(1)} collective-permute-done((f32[32,2,8,256]{3,2,1,0:T(8,128)S(1)}, f32[32,2,8,256]{3,2,1,0:T(8,128)S(1)}, u32[]{:S(2)}, u32[]{:S(2)}) %collective-permute-start.1) | collective-permute-done | bytes 524320 | tf_op jit(solution)/shard_map/ppermute | solution.py:226
  62.8 0.0 copy-done
  62.8 0.0 copy-done.1
  62.8 0.0 copy-start.2
  62.8 0.8 %copy-done.2 = f32[32,2,8,256]{3,2,1,0:T(8,128)} copy-done((f32[32,2,8,256]{3,2,1,0:T(8,128)}, f32[32,2,8,256]{3,2,1,0:T(8,128)S(1)}, u32[]{:S(2)}) %copy-start.2) | copy-done | bytes 524312
  63.6 3.1 %shard_map.57 = f32[32,2,8,256]{3,2,1,0:T(8,128)} custom-call(s32[4]{0:T(128)} %shifts_ref.1, f32[4]{0:T(128)} %strengths_ref.1, f32[32,2,8,256]{3,2,1,0:T(8,128)} %copy-done.2, f32[32,2,8,256]{3,2,1,0:T(8,128)} %copy-done, f32[32,2,8,256]{3,2,1,0:T(8,128)} %copy-done.1), custom_call_target="tpu_custom_call" | custom-call | tf_op jit(solution)/shard_map/pallas_call | solution.py:229
Async XLA Ops:
  5.9 3.6 %collective-permute-start = (f32[256,256]{1,0:T(8,128)}, f32[256,256]{1,0:T(8,128)S(1)}, u32[]{:S(2)}, u32[]{:S(2)}) collective-permute-start(f32[256,256]{1,0:T(8,128)} %get-tuple-element.10.own_ref), channel_id=1, source_target_pairs={{0,1},{1,0},{2,3},{3,2},{4,5},{5,4},{6,7},{7,6},{8,9},{9,8},{10,11... | collective-permute-start | bytes 786440 | tf_op jit(solution)/shard_map/ppermute | solution.py:216
  9.6 0.7 %copy-start.3 = (f32[256,256]{1,0:T(8,128)}, f32[256,256]{1,0:T(8,128)S(1)}, u32[]{:S(2)}) copy-start(f32[256,256]{1,0:T(8,128)S(1)} %collective-permute-done.other_ref) | copy-start | bytes 786436
  42.5 20.3 %copy-start = (f32[32,2,8,256]{3,2,1,0:T(8,128)}, f32[32,2,8,256]{3,2,1,0:T(8,128)S(1)}, u32[]{:S(2)}) copy-start(f32[32,2,8,256]{3,2,1,0:T(8,128)S(1)} %all_to_all.5.own_ref) | copy-start | bytes 1572868
  42.5 16.1 %collective-permute-start.2 = (f32[32,2,8,256]{3,2,1,0:T(8,128)S(1)}, f32[32,2,8,256]{3,2,1,0:T(8,128)S(1)}, u32[]{:S(2)}, u32[]{:S(2)}) collective-permute-start(f32[32,2,8,256]{3,2,1,0:T(8,128)S(1)} %all_to_all.5.own_ref), channel_id=1, source_target_pairs={{64,0},{128,64},{192,128},{256,192},{320,256},{384,320},{448,384},... | collective-permute-start | bytes 1572872 | tf_op jit(solution)/shard_map/ppermute | solution.py:227
  47.2 15.5 %collective-permute-start.1 = (f32[32,2,8,256]{3,2,1,0:T(8,128)S(1)}, f32[32,2,8,256]{3,2,1,0:T(8,128)S(1)}, u32[]{:S(2)}, u32[]{:S(2)}) collective-permute-start(f32[32,2,8,256]{3,2,1,0:T(8,128)S(1)} %all_to_all.5.own_ref), channel_id=1, source_target_pairs={{0,64},{64,128},{128,192},{192,256},{256,320},{320,384},{384,448},... | collective-permute-start | bytes 1572872 | tf_op jit(solution)/shard_map/ppermute | solution.py:226
  58.6 4.1 %copy-start.1 = (f32[32,2,8,256]{3,2,1,0:T(8,128)}, f32[32,2,8,256]{3,2,1,0:T(8,128)S(1)}, u32[]{:S(2)}) copy-start(f32[32,2,8,256]{3,2,1,0:T(8,128)S(1)} %collective-permute-done.2.above_ref) | copy-start | bytes 1572868
  62.8 0.8 %copy-start.2 = (f32[32,2,8,256]{3,2,1,0:T(8,128)}, f32[32,2,8,256]{3,2,1,0:T(8,128)S(1)}, u32[]{:S(2)}) copy-start(f32[32,2,8,256]{3,2,1,0:T(8,128)S(1)} %collective-permute-done.1.below_ref) | copy-start | bytes 1572868
where the time goes:
time: 67 us; the launch traced here: 66.7 us
  blocking collectives  28.1 us (42%)
  waiting for transfers between devices  15.3 us (23%)
  Pallas kernels  13.2 us (20%)
  starting transfers between devices  8.54 us (13%)
  local copies, waits for them, and re-layouts  1.49 us (2%)
    all_to_all x1, blocking collectives, body(): lax.all_to_all(green, 'elem', split_axis=0, concat_axis=0, tiled=True)  28.1 us
    ppermute x1, waiting for transfers between devices, body(): above = lax.ppermute(arrived, 'energy', [(i + 1, i) for i in range(ends)])  9.48 us
    pallas_call x1, Pallas kernels, body(): pl.pallas_call(eliminate_kernel, out_shape=[square] * 5, in_specs=[vmem]...  5.94 us
    ppermute x1, starting transfers between devices, body(): above = lax.ppermute(arrived, 'energy', [(i + 1, i) for i in range(ends)])  4.71 us
    pallas_call x1, Pallas kernels, body(): pl.pallas_call(recover_kernel, out_shape=jax.ShapeDtypeStruct((elem_size,...  4.18 us
    ppermute x1, waiting for transfers between devices, body(): below = lax.ppermute(arrived, 'energy', [(i, i + 1) for i in range(ends)])  4.11 us
    pallas_call x1, Pallas kernels, body(): pl.pallas_call(spread_kernel, out_shape=jax.ShapeDtypeStruct(arrived.shap...  3.11 us
    ppermute x1, starting transfers between devices, body(): below = lax.ppermute(arrived, 'energy', [(i, i + 1) for i in range(ends)])  1.92 us
  transfers between devices with their start and end apart: 3, of which 3 were waited for; matrix products, arithmetic and copies ran while one was open for 0% of the time, Pallas kernels for 0%

commit v1 on v0

--- a/solution.py
+++ b/solution.py
@@ -8,8 +8,10 @@
 from jax.sharding import PartitionSpec as P
 
 MODES = 4
+STEPS = 4
 LEVEL_STEP = 3.0 / 384.0
 RESIDUAL_MAX = 1e-3
+VMEM_BYTES = 12 * 1024 * 1024
 
 f32 = jnp.float32
 bf16 = jnp.bfloat16
@@ -21,7 +23,14 @@
 
 
 def product_1(left, right):
-    return jnp.dot(left, right, preferred_element_type=f32)
+    half = left.shape[0] // 2
+    return jnp.concatenate(
+        [
+            jnp.dot(rows, right, preferred_element_type=f32)
+            for rows in (left[:half], left[half:])
+        ],
+        axis=0,
+    )
 
 
 def product_3(left, right):
@@ -40,13 +49,15 @@
     return rows == columns
 
 
-def invert_series(matrix, diagonal):
+def invert_series(matrix, diagonal, started=None):
     size = matrix.shape[0]
     mass = jnp.sum(jnp.where(diagonal, matrix, 0.0), axis=0, keepdims=True)
     scale = size / jnp.sum(mass, axis=1, keepdims=True)
     one = jnp.where(diagonal, 1.0, 0.0).astype(f32)
     rest = one - matrix * scale
     rest_parts = parts_of(rest)
+    if started is not None:
+        started()
     rest_2 = product_1(rest_parts[0], rest_parts[0])
     rest_2b = rest_2.astype(bf16)
     rest_3 = product_1(rest_parts[0], rest_2b)
@@ -89,9 +100,36 @@
 
 
 def eliminate_kernel(
-    cell_ref, coupling_ref, sigma_ref, sum_ref, first_ref, fold_ref, second_ref, far_ref, work
+    cell_hbm,
+    coupling_hbm,
+    sigma_hbm,
+    sum_ref,
+    first_ref,
+    fold_ref,
+    second_ref,
+    far_ref,
+    cell_ref,
+    coupling_ref,
+    sigma_ref,
+    work,
+    sems,
 ):
     part = lax.axis_index("space")
+    copies = [
+        pltpu.make_async_copy(source.at[index], target.at[index], sems.at[number])
+        for number, (source, target, index) in enumerate(
+            (
+                (cell_hbm, cell_ref, part),
+                (sigma_hbm.at[0], sigma_ref, part),
+                (coupling_hbm, coupling_ref, part),
+                (cell_hbm, cell_ref, 1 - part),
+                (sigma_hbm.at[0], sigma_ref, 1 - part),
+                (coupling_hbm, coupling_ref, 1 - part),
+            )
+        )
+    ]
+    for copy in copies:
+        copy.start()
     position = lax.axis_index("energy") * lax.axis_size("elem") + lax.axis_index("elem")
     level = position.astype(f32) * LEVEL_STEP
     near = part == 0
@@ -99,10 +137,15 @@
     diagonal = diagonal_mask(size)
 
     def block(index):
-        return cell_ref[index] + jnp.where(diagonal, level, 0.0) + sigma_ref[0, index].astype(f32)
-
-    def chain(invert, product, parts):
-        outer, inner, last = (block(part), block(0), block(1))
+        return cell_ref[index] + jnp.where(diagonal, level, 0.0) + sigma_ref[index].astype(f32)
+
+    def arrive():
+        for copy in copies[2:]:
+            copy.wait()
+
+    def chain(invert_outer, invert, product, parts):
+        first, error = invert_outer(block(part))
+        inner, last = (block(0), block(1))
         link = coupling_ref[part]
         link_turned = link.T
         link, link_turned = (
@@ -113,7 +156,6 @@
         inner_link, inner_turned = (
             jnp.where(near, inner_link, inner_turned), jnp.where(near, inner_turned, inner_link)
         )
-        first, error = invert(outer)
         fold = product(parts(first), parts(link))
         second, error_second = invert(inner - product(parts(link_turned), parts(fold)))
         far = product(parts(second), parts(inner_link))
@@ -125,15 +167,19 @@
         sum_ref[...] = total
         return jnp.maximum(error, error_second)
 
-    error = chain(lambda m: invert_series(m, diagonal), product_3, parts_of)
+    for copy in copies[:2]:
+        copy.wait()
+    error = chain(
+        lambda m: invert_series(m, diagonal, arrive),
+        lambda m: invert_series(m, diagonal),
+        product_3,
+        parts_of,
+    )
 
     @pl.when(jnp.logical_not(error[0, 0] <= RESIDUAL_MAX))
     def _():
-        chain(
-            lambda m: (invert_direct(m, diagonal, work), jnp.zeros((1, 1), f32)),
-            product_full,
-            lambda m: m,
-        )
+        direct = lambda m: (invert_direct(m, diagonal, work), jnp.zeros((1, 1), f32))
+        chain(direct, direct, product_full, lambda m: m)
 
 
 def recover_kernel(own_ref, other_ref, first_ref, fold_ref, second_ref, far_ref, green_ref, work):
@@ -176,27 +222,45 @@
         )
 
 
-def spread_kernel(shifts_ref, strengths_ref, below_ref, own_ref, above_ref, out_ref, rim, sems):
+def inner_kernel(shifts_ref, strengths_ref, own_ref, out_ref):
     width = own_ref.shape[0]
-    copies = [
-        pltpu.make_async_copy(source, rim.at[pl.ds(place * width, width)], sems.at[place])
-        for place, source in enumerate((below_ref, own_ref, above_ref))
-    ]
-    for copy in copies:
-        copy.start()
-    for copy in copies:
-        copy.wait()
 
     def one(index, _):
         total = None
         for phonon in range(MODES):
-            shift = shifts_ref[phonon]
-            term = strengths_ref[phonon] * (rim[width + index - shift] + rim[width + index + shift])
+            low, high = (index - shifts_ref[phonon], index + shifts_ref[phonon])
+            strength = strengths_ref[phonon]
+            term = jnp.where(low >= 0, strength, 0.0) * own_ref[jnp.maximum(low, 0)]
+            term += jnp.where(high < width, strength, 0.0) * own_ref[jnp.minimum(high, width - 1)]
             total = term if total is None else total + term
         out_ref[index] = total
         return 0
 
     lax.fori_loop(0, width, one, 0, unroll=4)
+
+
+def outer_kernel(shifts_ref, strengths_ref, inner_ref, below_ref, above_ref, out_ref):
+    width = below_ref.shape[0]
+    span = out_ref.shape[0]
+    start = pl.program_id(0) * span
+
+    def one(step, _):
+        index = start + step
+        total = inner_ref[step]
+        for phonon in range(MODES):
+            low, high = (index - shifts_ref[phonon], index + shifts_ref[phonon])
+            strength = strengths_ref[phonon]
+            total += (
+                jnp.where(low < 0, strength, 0.0)
+                * below_ref[jnp.minimum(low + width, width - 1)]
+            )
+            total += (
+                jnp.where(high >= width, strength, 0.0) * above_ref[jnp.maximum(high - width, 0)]
+            )
+        out_ref[step] = total
+        return 0
+
+    lax.fori_loop(0, span, one, 0, unroll=4)
 
 
 def body(cell_blocks, coupling_blocks, sigma_prev, shifts, strengths):
@@ -205,14 +269,24 @@
     square = jax.ShapeDtypeStruct((orbitals, orbitals), f32)
     vmem = pl.BlockSpec(memory_space=pltpu.VMEM)
     smem = pl.BlockSpec(memory_space=pltpu.SMEM)
-    anywhere = pl.BlockSpec(memory_space=pl.ANY)
+    hbm = pl.BlockSpec(memory_space=pltpu.HBM)
     own, first, fold, second, far = pl.pallas_call(
         eliminate_kernel,
         out_shape=[square] * 5,
-        in_specs=[vmem] * 3,
+        in_specs=[hbm] * 3,
         out_specs=[vmem] * 5,
-        scratch_shapes=[pltpu.VMEM((orbitals, orbitals), f32)],
-    )(cell_blocks, coupling_blocks, sigma_prev)
+        scratch_shapes=[
+            pltpu.VMEM(cell_blocks.shape, f32),
+            pltpu.VMEM(coupling_blocks.shape, f32),
+            pltpu.VMEM(sigma_prev.shape[1:], sigma_prev.dtype),
+            pltpu.VMEM((orbitals, orbitals), f32),
+            pltpu.SemaphoreType.DMA((6,)),
+        ],
+        compiler_params=pltpu.CompilerParams(vmem_limit_bytes=VMEM_BYTES),
+    )(*(
+        pltpu.with_memory_space_constraint(argument, pltpu.HBM)
+        for argument in (cell_blocks, coupling_blocks, sigma_prev)
+    ))
     other = lax.ppermute(own, "space", [(0, 1), (1, 0)])
     green = pl.pallas_call(
         recover_kernel,
@@ -220,22 +294,32 @@
         in_specs=[vmem] * 6,
         out_specs=vmem,
         scratch_shapes=[pltpu.VMEM((orbitals, orbitals), f32)],
+        compiler_params=pltpu.CompilerParams(vmem_limit_bytes=VMEM_BYTES),
     )(own, other, first, fold, second, far)
     arrived = lax.all_to_all(green, "elem", split_axis=0, concat_axis=0, tiled=True)
     ends = lax.axis_size("energy") - 1
     below = lax.ppermute(arrived, "energy", [(i, i + 1) for i in range(ends)])
     above = lax.ppermute(arrived, "energy", [(i + 1, i) for i in range(ends)])
-    width = arrived.shape[0]
+    limits = pltpu.CompilerParams(vmem_limit_bytes=VMEM_BYTES)
+    inner = pl.pallas_call(
+        inner_kernel,
+        out_shape=jax.ShapeDtypeStruct(arrived.shape, f32),
+        in_specs=[smem, smem, vmem],
+        out_specs=vmem,
+        compiler_params=limits,
+        cost_estimate=pl.CostEstimate(
+            flops=16 * arrived.size, bytes_accessed=8 * arrived.size, transcendentals=0
+        ),
+    )(shifts, strengths, arrived)
+    piece = pl.BlockSpec((arrived.shape[0] // STEPS,) + arrived.shape[1:], lambda i: (i, 0, 0, 0))
     return pl.pallas_call(
-        spread_kernel,
+        outer_kernel,
+        grid=(STEPS,),
         out_shape=jax.ShapeDtypeStruct(arrived.shape, f32),
-        in_specs=[smem, smem, anywhere, anywhere, anywhere],
-        out_specs=vmem,
-        scratch_shapes=[
-            pltpu.VMEM((3 * width,) + arrived.shape[1:], f32),
-            pltpu.SemaphoreType.DMA((3,)),
-        ],
-    )(shifts, strengths, below, arrived, above)
+        in_specs=[smem, smem, piece, vmem, vmem],
+        out_specs=piece,
+        compiler_params=limits,
+    )(shifts, strengths, inner, below, above)
 
 
 def solution(mesh):

time: 67 us -> 61.8 us (0.922)
  the two profiles are of different devices: /device:TPU:66 before, /device:TPU:192 now
where the time goes in v1:
time: 61.8 us; the launch traced here: 61.6 us
  blocking collectives  28.2 us (46%)
  waiting for transfers between devices  14.1 us (23%)
  Pallas kernels  9.96 us (16%)
  starting transfers between devices  9.33 us (15%)
    all_to_all x1, blocking collectives, body(): lax.all_to_all(green, 'elem', split_axis=0, concat_axis=0, tiled=True)  28.2 us
    ppermute x1, waiting for transfers between devices, body(): below = lax.ppermute(arrived, 'energy', [(i, i + 1) for i in range(ends)])  7.23 us
    ppermute x1, starting transfers between devices, body(): below = lax.ppermute(arrived, 'energy', [(i, i + 1) for i in range(ends)])  5.49 us
    ppermute x1, waiting for transfers between devices, body(): above = lax.ppermute(arrived, 'energy', [(i + 1, i) for i in range(ends)])  5.33 us
    pallas_call x1, Pallas kernels, body(): pl.pallas_call(eliminate_kernel, out_shape=[square] * 5, in_specs=[hbm] *...  4.48 us
    pallas_call x1, Pallas kernels, body(): pl.pallas_call(outer_kernel, grid=(STEPS,), out_shape=jax.ShapeDtypeStruc...  2.44 us
    ppermute x1, starting transfers between devices, body(): above = lax.ppermute(arrived, 'energy', [(i + 1, i) for i in range(ends)])  1.92 us
    ppermute x1, starting transfers between devices, body(): other = lax.ppermute(own, 'space', [(0, 1), (1, 0)])  1.92 us
  transfers between devices with their start and end apart: 3, of which 3 were waited for; matrix products, arithmetic and copies ran while one was open for 0% of the time, Pallas kernels for 2%

profile of v1, /device:TPU:192, one launch (start us, length us, event | category | flops | bytes accessed | tf_op | source)
XLA Modules:
  0.0 61.6 jit_solution(11480664113897493098)
XLA Ops:
  0.0 4.5 %shard_map.55 = (f32[256,256]{1,0:T(8,128)S(1)}, f32[256,256]{1,0:T(8,128)S(1)}, f32[256,256]{1,0:T(8,128)S(1)}, f32[256,256]{1,0:T(8,128)S(1)}, f32[256,256]{1,0:T(8,128)S(1)}) custom-call(f32[2,256,256]{2,1,0:T(8,128)} %cell_hbm.1, f32[2,256,256]{2,1,0:T(8,128)} %coupling_hbm.1, bf16[1,2,256,256]{3,2,1,0:T(8,128)(2,1)} %sigma_hbm.1), custom_call_target="tpu_custom_call" | custom-call | tf_op jit(solution)/shard_map/pallas_call | solution.py:273
  4.5 1.9 %collective-permute-start = (f32[256,256]{1,0:T(8,128)S(1)}, f32[256,256]{1,0:T(8,128)S(1)}, u32[]{:S(2)}, u32[]{:S(2)}) collective-permute-start(f32[256,256]{1,0:T(8,128)S(1)} %get-tuple-element.10.own_ref), channel_id=1, source_target_pairs={{0,1},{1,0},{2,3},{3,2},{4,5},{5,4},{6,7},{7,6},{8,9},{9,8},{10,11... | collective-permute-start | bytes 786440 | tf_op jit(solution)/shard_map/ppermute | solution.py:290
  6.4 1.5 %collective-permute-done.other_ref = f32[256,256]{1,0:T(8,128)S(1)} collective-permute-done((f32[256,256]{1,0:T(8,128)S(1)}, f32[256,256]{1,0:T(8,128)S(1)}, u32[]{:S(2)}, u32[]{:S(2)}) %collective-permute-start) | collective-permute-done | bytes 262176 | tf_op jit(solution)/shard_map/ppermute | solution.py:290
  7.9 1.9 %shard_map.56 = f32[32,2,8,256]{3,2,1,0:T(8,128)S(1)} custom-call(f32[256,256]{1,0:T(8,128)S(1)} %get-tuple-element.10.own_ref, f32[256,256]{1,0:T(8,128)S(1)} %collective-permute-done.other_ref, f32[256,256]{1,0:T(8,128)S(1)} %get-tuple-element.11.first_ref, f32[256,256]{1,0:T(8,128)S(1)} %get-tuple-element.12.fold_ref, ...), custom_call_target="tpu_custom_call" | custom-call | tf_op jit(solution)/shard_map/pallas_call | solution.py:291
  9.8 0.0 copy-start
  9.8 0.0 copy-start.1
  9.8 28.2 %all_to_all.5.own_ref = f32[32,2,8,256]{3,2,1,0:T(8,128)S(1)} all-to-all(f32[32,2,8,256]{3,2,1,0:T(8,128)S(1)} %shard_map.56), channel_id=1, replica_groups=mesh['energy'=12,'elem'=32,'space'=2] {'elem'}, dimensions={0} | all-to-all | bytes 1048576 | tf_op jit(solution)/shard_map/all_to_all | solution.py:299
  38.0 5.5 %collective-permute-start.1 = (f32[32,2,8,256]{3,2,1,0:T(8,128)S(1)}, f32[32,2,8,256]{3,2,1,0:T(8,128)S(1)}, u32[]{:S(2)}, u32[]{:S(2)}) collective-permute-start(f32[32,2,8,256]{3,2,1,0:T(8,128)S(1)} %all_to_all.5.own_ref), channel_id=1, source_target_pairs={{0,64},{64,128},{128,192},{192,256},{256,320},{320,384},{384,448},... | collective-permute-start | bytes 1572872 | tf_op jit(solution)/shard_map/ppermute | solution.py:301
  43.5 1.9 %collective-permute-start.2 = (f32[32,2,8,256]{3,2,1,0:T(8,128)S(1)}, f32[32,2,8,256]{3,2,1,0:T(8,128)S(1)}, u32[]{:S(2)}, u32[]{:S(2)}) collective-permute-start(f32[32,2,8,256]{3,2,1,0:T(8,128)S(1)} %all_to_all.5.own_ref), channel_id=1, source_target_pairs={{64,0},{128,64},{192,128},{256,192},{320,256},{384,320},{448,384},... | collective-permute-start | bytes 1572872 | tf_op jit(solution)/shard_map/ppermute | solution.py:302
  45.4 0.0 copy-done
  45.5 0.0 copy-done.1
  45.5 1.1 %shard_map.57.inner_ref = f32[32,2,8,256]{3,2,1,0:T(8,128)S(1)} custom-call(s32[4]{0:T(128)S(1)} %copy-done, f32[4]{0:T(128)S(1)} %copy-done.1, f32[32,2,8,256]{3,2,1,0:T(8,128)S(1)} %all_to_all.5.own_ref), custom_call_target="tpu_custom_call" | custom-call | flops 2097152 | bytes 1048576 | tf_op jit(solution)/shard_map/pallas_call | solution.py:304
  46.6 7.2 %collective-permute-done.1.below_ref = f32[32,2,8,256]{3,2,1,0:T(8,128)S(1)} collective-permute-done((f32[32,2,8,256]{3,2,1,0:T(8,128)S(1)}, f32[32,2,8,256]{3,2,1,0:T(8,128)S(1)}, u32[]{:S(2)}, u32[]{:S(2)}) %collective-permute-start.1) | collective-permute-done | bytes 524320 | tf_op jit(solution)/shard_map/ppermute | solution.py:301
  53.8 5.3 %collective-permute-done.2.above_ref = f32[32,2,8,256]{3,2,1,0:T(8,128)S(1)} collective-permute-done((f32[32,2,8,256]{3,2,1,0:T(8,128)S(1)}, f32[32,2,8,256]{3,2,1,0:T(8,128)S(1)}, u32[]{:S(2)}, u32[]{:S(2)}) %collective-permute-start.2) | collective-permute-done | bytes 524320 | tf_op jit(solution)/shard_map/ppermute | solution.py:302
  59.2 2.4 %shard_map.58 = f32[32,2,8,256]{3,2,1,0:T(8,128)} custom-call(s32[4]{0:T(128)S(1)} %copy-done, f32[4]{0:T(128)S(1)} %copy-done.1, f32[32,2,8,256]{3,2,1,0:T(8,128)S(1)} %shard_map.57.inner_ref, f32[32,2,8,256]{3,2,1,0:T(8,128)S(1)} %collective-permute-done.1.below_ref, f32[32,2,8,256]{3,2,1,0:T(8,128)S(1)} %collective-permute-done.2.above_ref), custom_call_target="tpu_custom_call" | custom-call | tf_op jit(solution)/shard_map/pallas_call | solution.py:315
Async XLA Ops:
  4.5 3.4 %collective-permute-start = (f32[256,256]{1,0:T(8,128)S(1)}, f32[256,256]{1,0:T(8,128)S(1)}, u32[]{:S(2)}, u32[]{:S(2)}) collective-permute-start(f32[256,256]{1,0:T(8,128)S(1)} %get-tuple-element.10.own_ref), channel_id=1, source_target_pairs={{0,1},{1,0},{2,3},{3,2},{4,5},{5,4},{6,7},{7,6},{8,9},{9,8},{10,11... | collective-permute-start | bytes 786440 | tf_op jit(solution)/shard_map/ppermute | solution.py:290
  9.8 35.6 %copy-start = (s32[4]{0:T(128)S(1)}, s32[4]{0:T(128)}, u32[]{:S(2)}) copy-start(s32[4]{0:T(128)} %shifts_ref.3) | copy-start | bytes 52
  9.8 35.6 %copy-start.1 = (f32[4]{0:T(128)S(1)}, f32[4]{0:T(128)}, u32[]{:S(2)}) copy-start(f32[4]{0:T(128)} %strengths_ref.3) | copy-start | bytes 52
  38.0 15.8 %collective-permute-start.1 = (f32[32,2,8,256]{3,2,1,0:T(8,128)S(1)}, f32[32,2,8,256]{3,2,1,0:T(8,128)S(1)}, u32[]{:S(2)}, u32[]{:S(2)}) collective-permute-start(f32[32,2,8,256]{3,2,1,0:T(8,128)S(1)} %all_to_all.5.own_ref), channel_id=1, source_target_pairs={{0,64},{64,128},{128,192},{192,256},{256,320},{320,384},{384,448},... | collective-permute-start | bytes 1572872 | tf_op jit(solution)/shard_map/ppermute | solution.py:301
  43.5 15.7 %collective-permute-start.2 = (f32[32,2,8,256]{3,2,1,0:T(8,128)S(1)}, f32[32,2,8,256]{3,2,1,0:T(8,128)S(1)}, u32[]{:S(2)}, u32[]{:S(2)}) collective-permute-start(f32[32,2,8,256]{3,2,1,0:T(8,128)S(1)} %all_to_all.5.own_ref), channel_id=1, source_target_pairs={{64,0},{128,64},{192,128},{256,192},{320,256},{384,320},{448,384},... | collective-permute-start | bytes 1572872 | tf_op jit(solution)/shard_map/ppermute | solution.py:302

commit v2 on v1

--- a/solution.py
+++ b/solution.py
@@ -8,7 +8,7 @@
 from jax.sharding import PartitionSpec as P
 
 MODES = 4
-STEPS = 4
+STEPS = 2
 LEVEL_STEP = 3.0 / 384.0
 RESIDUAL_MAX = 1e-3
 VMEM_BYTES = 12 * 1024 * 1024
@@ -34,9 +34,18 @@
 
 
 def product_3(left, right):
-    return product_1(left[0], right[0]) + (
-        product_1(left[1], right[0]) + product_1(left[0], right[1])
-    )
+    half = left[0].shape[0] // 2
+    results = []
+    for rows in (slice(0, half), slice(half, None)):
+        both = jnp.dot(
+            jnp.concatenate([left[0][rows], left[1][rows]], axis=0),
+            right[0],
+            preferred_element_type=f32,
+        )
+        results.append(
+            both[:half] + (both[half:] + jnp.dot(left[0][rows], right[1], preferred_element_type=f32))
+        )
+    return jnp.concatenate(results, axis=0)
 
 
 def product_full(left, right):
@@ -222,45 +231,28 @@
         )
 
 
-def inner_kernel(shifts_ref, strengths_ref, own_ref, out_ref):
+def spread_kernel(
+    shifts_ref, strengths_ref, below_ref, own_ref, above_ref, out_hbm, rim, out_ref, sems
+):
     width = own_ref.shape[0]
-
-    def one(index, _):
-        total = None
-        for phonon in range(MODES):
-            low, high = (index - shifts_ref[phonon], index + shifts_ref[phonon])
-            strength = strengths_ref[phonon]
-            term = jnp.where(low >= 0, strength, 0.0) * own_ref[jnp.maximum(low, 0)]
-            term += jnp.where(high < width, strength, 0.0) * own_ref[jnp.minimum(high, width - 1)]
-            total = term if total is None else total + term
-        out_ref[index] = total
-        return 0
-
-    lax.fori_loop(0, width, one, 0, unroll=4)
-
-
-def outer_kernel(shifts_ref, strengths_ref, inner_ref, below_ref, above_ref, out_ref):
-    width = below_ref.shape[0]
-    span = out_ref.shape[0]
-    start = pl.program_id(0) * span
-
-    def one(step, _):
-        index = start + step
-        total = inner_ref[step]
-        for phonon in range(MODES):
-            low, high = (index - shifts_ref[phonon], index + shifts_ref[phonon])
-            strength = strengths_ref[phonon]
-            total += (
-                jnp.where(low < 0, strength, 0.0)
-                * below_ref[jnp.minimum(low + width, width - 1)]
-            )
-            total += (
-                jnp.where(high >= width, strength, 0.0) * above_ref[jnp.maximum(high - width, 0)]
-            )
-        out_ref[step] = total
-        return 0
-
-    lax.fori_loop(0, span, one, 0, unroll=4)
+    span = width // STEPS
+    for place, source in enumerate((below_ref, own_ref, above_ref)):
+        rim[place * width : (place + 1) * width] = source[...]
+    shifts = [shifts_ref[phonon] for phonon in range(MODES)]
+    strengths = [strengths_ref[phonon] for phonon in range(MODES)]
+    copies = []
+    for step in range(STEPS):
+        for index in range(step * span, (step + 1) * span):
+            total = None
+            for shift, strength in zip(shifts, strengths):
+                term = strength * (rim[width + index - shift] + rim[width + index + shift])
+                total = term if total is None else total + term
+            out_ref[index] = total
+        piece = pl.ds(step * span, span)
+        copies.append(pltpu.make_async_copy(out_ref.at[piece], out_hbm.at[piece], sems.at[step]))
+        copies[-1].start()
+    for copy in copies:
+        copy.wait()
 
 
 def body(cell_blocks, coupling_blocks, sigma_prev, shifts, strengths):
@@ -300,26 +292,19 @@
     ends = lax.axis_size("energy") - 1
     below = lax.ppermute(arrived, "energy", [(i, i + 1) for i in range(ends)])
     above = lax.ppermute(arrived, "energy", [(i + 1, i) for i in range(ends)])
-    limits = pltpu.CompilerParams(vmem_limit_bytes=VMEM_BYTES)
-    inner = pl.pallas_call(
-        inner_kernel,
+    width = arrived.shape[0]
+    return pl.pallas_call(
+        spread_kernel,
         out_shape=jax.ShapeDtypeStruct(arrived.shape, f32),
-        in_specs=[smem, smem, vmem],
-        out_specs=vmem,
-        compiler_params=limits,
-        cost_estimate=pl.CostEstimate(
-            flops=16 * arrived.size, bytes_accessed=8 * arrived.size, transcendentals=0
-        ),
-    )(shifts, strengths, arrived)
-    piece = pl.BlockSpec((arrived.shape[0] // STEPS,) + arrived.shape[1:], lambda i: (i, 0, 0, 0))
-    return pl.pallas_call(
-        outer_kernel,
-        grid=(STEPS,),
-        out_shape=jax.ShapeDtypeStruct(arrived.shape, f32),
-        in_specs=[smem, smem, piece, vmem, vmem],
-        out_specs=piece,
-        compiler_params=limits,
-    )(shifts, strengths, inner, below, above)
+        in_specs=[smem, smem, vmem, vmem, vmem],
+        out_specs=hbm,
+        scratch_shapes=[
+            pltpu.VMEM((3 * width,) + arrived.shape[1:], f32),
+            pltpu.VMEM(arrived.shape, f32),
+            pltpu.SemaphoreType.DMA((STEPS,)),
+        ],
+        compiler_params=pltpu.CompilerParams(vmem_limit_bytes=VMEM_BYTES),
+    )(shifts, strengths, below, arrived, above)
 
 
 def solution(mesh):

time: 61.8 us -> 59.1 us (0.956)
  the two profiles are of different devices: /device:TPU:192 before, /device:TPU:512 now
where the time goes in v2:
time: 59.1 us; the launch traced here: 58.9 us
  blocking collectives  28.2 us (48%)
  waiting for transfers between devices  15 us (25%)
  Pallas kernels  7.86 us (13%)
  starting transfers between devices  7.75 us (13%)
    all_to_all x1, blocking collectives, body(): lax.all_to_all(green, 'elem', split_axis=0, concat_axis=0, tiled=True)  28.2 us
    ppermute x1, waiting for transfers between devices, body(): above = lax.ppermute(arrived, 'energy', [(i + 1, i) for i in range(ends)])  8.87 us
    ppermute x1, waiting for transfers between devices, body(): below = lax.ppermute(arrived, 'energy', [(i, i + 1) for i in range(ends)])  4.61 us
    pallas_call x1, Pallas kernels, body(): pl.pallas_call(eliminate_kernel, out_shape=[square] * 5, in_specs=[hbm] *...  4.43 us
    ppermute x1, starting transfers between devices, body(): above = lax.ppermute(arrived, 'energy', [(i + 1, i) for i in range(ends)])  3.66 us
    ppermute x1, starting transfers between devices, body(): below = lax.ppermute(arrived, 'energy', [(i, i + 1) for i in range(ends)])  2.17 us
    ppermute x1, starting transfers between devices, body(): other = lax.ppermute(own, 'space', [(0, 1), (1, 0)])  1.92 us
    pallas_call x1, Pallas kernels, body(): pl.pallas_call(recover_kernel, out_shape=jax.ShapeDtypeStruct((elem_size,...  1.86 us
  transfers between devices with their start and end apart: 3, of which 3 were waited for; matrix products, arithmetic and copies ran while one was open for 0% of the time, Pallas kernels for 0%

profile of v2, /device:TPU:512, one launch (start us, length us, event | category | flops | bytes accessed | tf_op | source)
XLA Modules:
  0.0 58.9 jit_solution(9642796693914873612)
XLA Ops:
  0.0 4.4 %shard_map.55 = (f32[256,256]{1,0:T(8,128)S(1)}, f32[256,256]{1,0:T(8,128)S(1)}, f32[256,256]{1,0:T(8,128)S(1)}, f32[256,256]{1,0:T(8,128)S(1)}, f32[256,256]{1,0:T(8,128)S(1)}) custom-call(f32[2,256,256]{2,1,0:T(8,128)} %cell_hbm.1, f32[2,256,256]{2,1,0:T(8,128)} %coupling_hbm.1, bf16[1,2,256,256]{3,2,1,0:T(8,128)(2,1)} %sigma_hbm.1), custom_call_target="tpu_custom_call" | custom-call | tf_op jit(solution)/shard_map/pallas_call | solution.py:265
  4.4 1.9 %collective-permute-start = (f32[256,256]{1,0:T(8,128)S(1)}, f32[256,256]{1,0:T(8,128)S(1)}, u32[]{:S(2)}, u32[]{:S(2)}) collective-permute-start(f32[256,256]{1,0:T(8,128)S(1)} %get-tuple-element.10.own_ref), channel_id=1, source_target_pairs={{0,1},{1,0},{2,3},{3,2},{4,5},{5,4},{6,7},{7,6},{8,9},{9,8},{10,11... | collective-permute-start | bytes 786440 | tf_op jit(solution)/shard_map/ppermute | solution.py:282
  6.4 1.5 %collective-permute-done.other_ref = f32[256,256]{1,0:T(8,128)S(1)} collective-permute-done((f32[256,256]{1,0:T(8,128)S(1)}, f32[256,256]{1,0:T(8,128)S(1)}, u32[]{:S(2)}, u32[]{:S(2)}) %collective-permute-start) | collective-permute-done | bytes 262176 | tf_op jit(solution)/shard_map/ppermute | solution.py:282
  7.9 1.9 %shard_map.56 = f32[32,2,8,256]{3,2,1,0:T(8,128)S(1)} custom-call(f32[256,256]{1,0:T(8,128)S(1)} %get-tuple-element.10.own_ref, f32[256,256]{1,0:T(8,128)S(1)} %collective-permute-done.other_ref, f32[256,256]{1,0:T(8,128)S(1)} %get-tuple-element.11.first_ref, f32[256,256]{1,0:T(8,128)S(1)} %get-tuple-element.12.fold_ref, ...), custom_call_target="tpu_custom_call" | custom-call | tf_op jit(solution)/shard_map/pallas_call | solution.py:283
  9.7 0.0 copy-start
  9.8 0.0 copy-start.1
  9.8 28.2 %all_to_all.5.own_ref = f32[32,2,8,256]{3,2,1,0:T(8,128)S(1)} all-to-all(f32[32,2,8,256]{3,2,1,0:T(8,128)S(1)} %shard_map.56), channel_id=1, replica_groups=mesh['energy'=12,'elem'=32,'space'=2] {'elem'}, dimensions={0} | all-to-all | bytes 1048576 | tf_op jit(solution)/shard_map/all_to_all | solution.py:291
  38.0 3.7 %collective-permute-start.2 = (f32[32,2,8,256]{3,2,1,0:T(8,128)S(1)}, f32[32,2,8,256]{3,2,1,0:T(8,128)S(1)}, u32[]{:S(2)}, u32[]{:S(2)}) collective-permute-start(f32[32,2,8,256]{3,2,1,0:T(8,128)S(1)} %all_to_all.5.own_ref), channel_id=1, source_target_pairs={{64,0},{128,64},{192,128},{256,192},{320,256},{384,320},{448,384},... | collective-permute-start | bytes 1572872 | tf_op jit(solution)/shard_map/ppermute | solution.py:294
  41.6 2.2 %collective-permute-start.1 = (f32[32,2,8,256]{3,2,1,0:T(8,128)S(1)}, f32[32,2,8,256]{3,2,1,0:T(8,128)S(1)}, u32[]{:S(2)}, u32[]{:S(2)}) collective-permute-start(f32[32,2,8,256]{3,2,1,0:T(8,128)S(1)} %all_to_all.5.own_ref), channel_id=1, source_target_pairs={{0,64},{64,128},{128,192},{192,256},{256,320},{320,384},{384,448},... | collective-permute-start | bytes 1572872 | tf_op jit(solution)/shard_map/ppermute | solution.py:293
  43.8 8.9 %collective-permute-done.2.above_ref = f32[32,2,8,256]{3,2,1,0:T(8,128)S(1)} collective-permute-done((f32[32,2,8,256]{3,2,1,0:T(8,128)S(1)}, f32[32,2,8,256]{3,2,1,0:T(8,128)S(1)}, u32[]{:S(2)}, u32[]{:S(2)}) %collective-permute-start.2) | collective-permute-done | bytes 524320 | tf_op jit(solution)/shard_map/ppermute | solution.py:294
  52.7 4.6 %collective-permute-done.1.below_ref = f32[32,2,8,256]{3,2,1,0:T(8,128)S(1)} collective-permute-done((f32[32,2,8,256]{3,2,1,0:T(8,128)S(1)}, f32[32,2,8,256]{3,2,1,0:T(8,128)S(1)}, u32[]{:S(2)}, u32[]{:S(2)}) %collective-permute-start.1) | collective-permute-done | bytes 524320 | tf_op jit(solution)/shard_map/ppermute | solution.py:293
  57.3 0.0 copy-done
  57.3 0.0 copy-done.1
  57.3 1.6 %shard_map.57 = f32[32,2,8,256]{3,2,1,0:T(8,128)} custom-call(s32[4]{0:T(128)S(1)} %copy-done, f32[4]{0:T(128)S(1)} %copy-done.1, f32[32,2,8,256]{3,2,1,0:T(8,128)S(1)} %collective-permute-done.1.below_ref, f32[32,2,8,256]{3,2,1,0:T(8,128)S(1)} %all_to_all.5.own_ref, f32[32,2,8,256]{3,2,1,0:T(8,128)S(1)} %collective-permute-done.2.above_ref), custom_call_target="tpu_custom_call" | custom-call | tf_op jit(solution)/shard_map/pallas_call | solution.py:296
Async XLA Ops:
  4.4 3.4 %collective-permute-start = (f32[256,256]{1,0:T(8,128)S(1)}, f32[256,256]{1,0:T(8,128)S(1)}, u32[]{:S(2)}, u32[]{:S(2)}) collective-permute-start(f32[256,256]{1,0:T(8,128)S(1)} %get-tuple-element.10.own_ref), channel_id=1, source_target_pairs={{0,1},{1,0},{2,3},{3,2},{4,5},{5,4},{6,7},{7,6},{8,9},{9,8},{10,11... | collective-permute-start | bytes 786440 | tf_op jit(solution)/shard_map/ppermute | solution.py:282
  9.7 47.5 %copy-start = (s32[4]{0:T(128)S(1)}, s32[4]{0:T(128)}, u32[]{:S(2)}) copy-start(s32[4]{0:T(128)} %shifts_ref.1) | copy-start | bytes 52
  9.8 47.5 %copy-start.1 = (f32[4]{0:T(128)S(1)}, f32[4]{0:T(128)}, u32[]{:S(2)}) copy-start(f32[4]{0:T(128)} %strengths_ref.1) | copy-start | bytes 52
  38.0 14.7 %collective-permute-start.2 = (f32[32,2,8,256]{3,2,1,0:T(8,128)S(1)}, f32[32,2,8,256]{3,2,1,0:T(8,128)S(1)}, u32[]{:S(2)}, u32[]{:S(2)}) collective-permute-start(f32[32,2,8,256]{3,2,1,0:T(8,128)S(1)} %all_to_all.5.own_ref), channel_id=1, source_target_pairs={{64,0},{128,64},{192,128},{256,192},{320,256},{384,320},{448,384},... | collective-permute-start | bytes 1572872 | tf_op jit(solution)/shard_map/ppermute | solution.py:294
  41.6 15.7 %collective-permute-start.1 = (f32[32,2,8,256]{3,2,1,0:T(8,128)S(1)}, f32[32,2,8,256]{3,2,1,0:T(8,128)S(1)}, u32[]{:S(2)}, u32[]{:S(2)}) collective-permute-start(f32[32,2,8,256]{3,2,1,0:T(8,128)S(1)} %all_to_all.5.own_ref), channel_id=1, source_target_pairs={{0,64},{64,128},{128,192},{192,256},{256,320},{320,384},{384,448},... | collective-permute-start | bytes 1572872 | tf_op jit(solution)/shard_map/ppermute | solution.py:293
